TPU v7x, 512 devices: a whole 4x8x8 slice. The times are simulated.
512 devices in a mesh: row: 32 (over z, x_lo, core), col: 16 (over y, x_hi).
Axes of the slice: x: 4 (x_hi: 2, x_lo: 2; x = x_hi * 2 + x_lo), y: 8, z: 8, core: 2. Of those that a mesh axis runs over, the one named last changes fastest.
Arguments:
- amplitudes: float32 [8192, 8192], P('row', 'col'), may hold values from -6 to 6
- factor: float32 [8192, 512], P('col'), may hold values from -1.2 to 1.2
- denominators: float32 [8192, 8192], P('row', 'col'), may hold values from 1 to 4
Outputs:
- new_amplitudes: float32 [8192, 8192], P('row', 'col')
All inputs are finite; a program needn't handle non-finite values.
Results may differ from a plain program's by a relative error of at most 0.0001.
Values sent between devices are 32-bit elements; how exact they have to be, the bound alone decides.
No kernel may reach another device: no remote copies, remote signals or barrier semaphores. Data moves between devices by JAX's collectives and lax.ppermute only.
A program may use at most 64 MiB of HBM per device.

v0:
```python
import math

import jax
import jax.numpy as jnp
from jax import lax
from jax.experimental import pallas as pl
from jax.experimental.pallas import tpu as pltpu
from jax.sharding import PartitionSpec as P

ITERS = 2
WIDE = 256
PAIR = 2
CORES = 2


def spread(block, axis, groups):
    return lax.all_to_all(block, axis, split_axis=0, concat_axis=0, axis_index_groups=groups, tiled=True)


def halves(x):
    high = x.astype(jnp.bfloat16)
    return high, (x - high.astype(jnp.float32)).astype(jnp.bfloat16)


def product(left, right, transposed):
    dims = (((1,), (1 if transposed else 0,)), ((), ()))

    def dot(a, b):
        return lax.dot_general(a, b, dims, preferred_element_type=jnp.float32)

    return dot(left[0], right[0]) + (dot(left[0], right[1]) + dot(left[1], right[0]))


def middle_kernel(scale, last, info, got, other, den, factor, out, rh, rl, ch, cl, ah, al):
    rows, thin = out.shape[0], got.shape[2]

    def sort(cols, mine, e):
        for j in range(got.shape[0]):
            here = slice(j * thin, (j + 1) * thin)
            rh[here, :], rl[here, :] = halves(mine[j, e])
            for f in range(CORES):
                there = slice(f * rows + j * thin, f * rows + (j + 1) * thin)
                ch[there, :], cl[there, :] = halves(cols[j, f])

    @pl.when(info[0] == 0)
    def _():
        sort(other, got, 0)

    @pl.when(info[0] == 1)
    def _():
        sort(got, other, 1)

    left = rh[...], rl[...]
    for at in range(0, ch.shape[0], WIDE):
        cols = slice(at, at + WIDE)
        amp = product(left, (ch[cols, :], cl[cols, :]), True) / den[:, cols]
        if last:
            out[:, cols] = amp
        else:
            ah[:, cols], al[:, cols] = halves(amp)
    if not last:
        left = ah[...], al[...]
        for at in range(0, out.shape[1], WIDE):
            cols = slice(at, at + WIDE)
            out[:, cols] = product(left, halves(factor[:, cols]), False) * scale

        @pl.when(info[1] == 1)
        def _():
            out[...] += factor[pl.ds(pl.multiple_of(info[0] * rows, rows), rows), :]


def middle_part(scale, last, info, got, other, den, factor):
    rows, cols = den.shape
    depth = factor.shape[1]
    vmem = pl.BlockSpec(memory_space=pltpu.VMEM)
    short = pltpu.VMEM((rows, depth), jnp.bfloat16)
    tall = pltpu.VMEM((cols, depth), jnp.bfloat16)
    wide = pltpu.VMEM((rows, cols), jnp.bfloat16)
    return pl.pallas_call(
        lambda *refs: middle_kernel(scale, last, *refs),
        out_shape=jax.ShapeDtypeStruct((rows, cols if last else depth), jnp.float32),
        in_specs=[pl.BlockSpec(memory_space=pltpu.SMEM), vmem, vmem, vmem, vmem],
        out_specs=vmem,
        scratch_shapes=[short, short, tall, tall, wide, wide],
        compiler_params=pltpu.CompilerParams(vmem_limit_bytes=20 << 20),
        cost_estimate=pl.CostEstimate(flops=12 * rows * depth * cols, bytes_accessed=4 << 20, transcendentals=0),
        name="last" if last else "middle",
    )(info, got, other, den, factor)


def local(amplitudes, factor, denominators):
    rows, depth = amplitudes.shape[0], factor.shape[1]
    nrow = lax.axis_size("row")
    ncol = lax.axis_size("col")
    line = ncol // PAIR
    thin = rows // ncol
    here_row = lax.axis_index("row")
    here_col = lax.axis_index("col")
    first = here_row % CORES == 0
    scale = 1.0 / math.sqrt(rows * nrow)
    info = jnp.stack([here_row % CORES, here_row // CORES == here_col]).astype(jnp.int32)
    team = [[k * CORES + e for e in range(CORES)] for k in range(ncol)]
    partner = [(r, r ^ 1) for r in range(nrow)]
    order = []
    for u in range(PAIR):
        for n in range(line):
            y = (n // 2 + (n + u) % 2 * (line // 2)) % line
            order.append(y * PAIR + u)
    place = [(c // PAIR + line // 2) % line * PAIR + c % PAIR for c in order]
    turn = [[] for _ in range(CORES)]
    for e in range(CORES):
        for c, q in zip(order, place):
            for k in range(ncol):
                turn[e].append(((k * CORES + e) * ncol + c, (q * CORES + 1) * ncol + k))
    both = [[k * CORES * ncol + c for c in order] for k in range(ncol)]
    both += [[(q * CORES + 1) * ncol + c for q in place] for c in range(ncol)]
    mine = lax.dynamic_slice_in_dim(factor, info[0] * rows, rows, 0)
    part = jnp.dot(amplitudes, factor, precision=lax.Precision.HIGH) * scale + jnp.where(info[1] == 1, mine, 0.0)
    for step in range(ITERS):
        terms = spread(part, "col", [order])
        piece = terms.reshape(ncol, thin, depth).sum(0)
        turned = []
        for e in range(CORES):
            turned.append(lax.ppermute(piece, ("row", "col"), turn[e]))
        pieces = lax.all_gather(piece, "row", axis=0, axis_index_groups=team, tiled=True)
        own = jnp.where(first, pieces, jnp.concatenate(turned))
        got = spread(jnp.tile(own, (ncol, 1)), ("row", "col"), both)
        other = lax.ppermute(got, "row", partner)
        got = got.reshape(ncol, CORES, thin, depth)
        other = other.reshape(ncol, CORES, thin, depth)
        part = middle_part(scale, step == ITERS - 1, info, got, other, denominators, factor)
    return part


def solution(mesh):
    return jax.shard_map(
        local,
        mesh=mesh,
        in_specs=(P("row", "col"), P("col", None), P("row", "col")),
        out_specs=P("row", "col"),
        check_vma=False,
    )
```

profile of v0, /device:TPU:1, one launch (start us, length us, event | category | flops | bytes accessed | tf_op | source)
XLA Modules:
  0.0 142.5 jit_solution(10763882789222319441)
XLA Ops:
  0.0 0.0 copy-start
  0.0 1.0 copy-done
  1.0 2.0 %fusion = f32[256,512]{1,0:T(8,128)S(1)} fusion(f32[256,512]{1,0:T(8,128)S(1)} %copy-done, f32[512,512]{1,0:T(8,128)} %refs_4_.3, s32[]{:T(128)S(6)} %select_n.40, pred[]{:T(512)S(6)} %eq.14), kind=kOutput, calls=%fused_computation.1 | convolution fusion | flops 403046400 | bytes 2621445 | tf_op jit(solution)/shard_map/dot_general | solution.py:118
  3.0 25.2 %all_to_all.36 = f32[16,16,512]{2,1,0:T(8,128)S(1)} all-to-all(f32[16,16,512]{2,1,0:T(8,128)S(1)} %bitcast.19), channel_id=1, replica_groups={{0,8,2,10,4,12,6,14,9,1,11,3,13,5,15,7},{16,24,18,26,20,28,22,30,25,17,..., dimensions={0} | all-to-all | bytes 1048576 | tf_op jit(solution)/shard_map/all_to_all | solution.py:17
  28.2 10.6 %collective-permute-start.1 = (f32[16,512]{1,0:T(8,128)S(1)}, f32[16,512]{1,0:T(8,128)S(1)}, u32[]{:S(2)}, u32[]{:S(2)}) collective-permute-start(f32[16,512]{1,0:T(8,128)S(1)} %reduce_sum.18), channel_id=1, source_target_pairs={{16,272},{48,273},{80,274},{112,275},{144,276},{176,277},{208,278}... | collective-permute-start | bytes 98312 | tf_op jit(solution)/shard_map/ppermute | solution.py:124
  38.9 1.3 collective-permute-start
  40.2 7.3 %all_gather.6 = f32[32,512]{1,0:T(8,128)S(1)} all-gather(f32[16,512]{1,0:T(8,128)S(1)} %reduce_sum.18), channel_id=1, replica_groups={{0,16},{32,48},{64,80},{96,112},{128,144},{160,176},{192,208},{224,240}..., dimensions={0}, use_global_device_ids=true | all-gather | bytes 98304 | tf_op jit(solution)/shard_map/all_gather | solution.py:125
  47.5 0.0 collective-permute-done.1
  47.5 0.7 collective-permute-done
  48.2 0.1 tile.4
  48.3 0.0 copy-start.1
  48.3 0.0 copy-start.2
  48.3 23.0 %all_to_all.37 = f32[16,32,512]{2,1,0:T(8,128)S(1)} all-to-all(f32[16,32,512]{2,1,0:T(8,128)S(1)} %tile.4), channel_id=1, replica_groups={{0,8,2,10,4,12,6,14,9,1,11,3,13,5,15,7},{32,40,34,42,36,44,38,46,41,33,..., dimensions={0} | all-to-all | bytes 2097152 | tf_op jit(solution)/shard_map/all_to_all | solution.py:17
  71.3 2.4 %collective-permute-start.2 = (f32[512,512]{1,0:T(8,128)S(1)}, f32[512,512]{1,0:T(8,128)S(1)}, u32[]{:S(2)}, u32[]{:S(2)}) collective-permute-start(f32[512,512]{1,0:T(8,128)S(1)} %bitcast.12), channel_id=1, source_target_pairs={{0,16},{16,0},{32,48},{48,32},{64,80},{80,64},{96,112},{112,96},{1... | collective-permute-start | bytes 3145736 | tf_op jit(solution)/shard_map/ppermute | solution.py:128
  73.7 0.1 pad_add_fusion.refs_0_
  73.8 2.2 %collective-permute-done.2 = f32[512,512]{1,0:T(8,128)S(1)} collective-permute-done((f32[512,512]{1,0:T(8,128)S(1)}, f32[512,512]{1,0:T(8,128)S(1)}, u32[]{:S(2)}, u32[]{:S(2)}) %collective-permute-start.2) | collective-permute-done | bytes 1048608 | tf_op jit(solution)/shard_map/ppermute | solution.py:128
  76.0 0.0 copy-done.1
  76.0 0.0 copy-done.2
  76.0 1.9 %middle.1 = f32[256,512]{1,0:T(8,128)S(1)} custom-call(s32[2]{0:T(128)S(1)} %pad_add_fusion.refs_0_, f32[16,2,16,512]{3,2,1,0:T(8,128)S(1)} %bitcast.13, f32[16,2,16,512]{3,2,1,0:T(8,128)S(1)} %bitcast.17, f32[256,512]{1,0:T(8,128)S(1)} %copy-done.2, f32[512,512]{1,0:T(8,128)S(1)} %copy-done.1), custom_call_target="tpu_custom_call" | custom-call | flops 805306368 | bytes 4194304 | tf_op jit(solution)/shard_map/middle/pallas_call | solution.py:79
  77.9 20.3 %all_to_all.38 = f32[16,16,512]{2,1,0:T(8,128)S(1)} all-to-all(f32[16,16,512]{2,1,0:T(8,128)S(1)} %bitcast.16), channel_id=1, replica_groups={{0,8,2,10,4,12,6,14,9,1,11,3,13,5,15,7},{16,24,18,26,20,28,22,30,25,17,..., dimensions={0} | all-to-all | bytes 1048576 | tf_op jit(solution)/shard_map/all_to_all | solution.py:17
  98.3 5.6 %collective-permute-start.4 = (f32[16,512]{1,0:T(8,128)S(1)}, f32[16,512]{1,0:T(8,128)S(1)}, u32[]{:S(2)}, u32[]{:S(2)}) collective-permute-start(f32[16,512]{1,0:T(8,128)S(1)} %reduce_sum.19), channel_id=1, source_target_pairs={{16,272},{48,273},{80,274},{112,275},{144,276},{176,277},{208,278}... | collective-permute-start | bytes 98312 | tf_op jit(solution)/shard_map/ppermute | solution.py:124
  103.9 1.3 collective-permute-start.3
  105.2 7.0 %all_gather.7 = f32[32,512]{1,0:T(8,128)S(1)} all-gather(f32[16,512]{1,0:T(8,128)S(1)} %reduce_sum.19), channel_id=1, replica_groups={{0,16},{32,48},{64,80},{96,112},{128,144},{160,176},{192,208},{224,240}..., dimensions={0}, use_global_device_ids=true | all-gather | bytes 98304 | tf_op jit(solution)/shard_map/all_gather | solution.py:125
  112.2 0.0 collective-permute-done.4
  112.2 0.8 collective-permute-done.3
  113.1 0.1 tile.5
  113.2 22.6 %all_to_all.39 = f32[16,32,512]{2,1,0:T(8,128)S(1)} all-to-all(f32[16,32,512]{2,1,0:T(8,128)S(1)} %tile.5), channel_id=1, replica_groups={{0,8,2,10,4,12,6,14,9,1,11,3,13,5,15,7},{32,40,34,42,36,44,38,46,41,33,..., dimensions={0} | all-to-all | bytes 2097152 | tf_op jit(solution)/shard_map/all_to_all | solution.py:17
  135.8 1.9 %collective-permute-start.5 = (f32[512,512]{1,0:T(8,128)S(1)}, f32[512,512]{1,0:T(8,128)S(1)}, u32[]{:S(2)}, u32[]{:S(2)}) collective-permute-start(f32[512,512]{1,0:T(8,128)S(1)} %bitcast.14), channel_id=1, source_target_pairs={{0,16},{16,0},{32,48},{48,32},{64,80},{80,64},{96,112},{112,96},{1... | collective-permute-start | bytes 3145736 | tf_op jit(solution)/shard_map/ppermute | solution.py:128
  137.8 2.6 %collective-permute-done.5 = f32[512,512]{1,0:T(8,128)S(1)} collective-permute-done((f32[512,512]{1,0:T(8,128)S(1)}, f32[512,512]{1,0:T(8,128)S(1)}, u32[]{:S(2)}, u32[]{:S(2)}) %collective-permute-start.5) | collective-permute-done | bytes 1048608 | tf_op jit(solution)/shard_map/ppermute | solution.py:128
  140.4 2.1 %last.1 = f32[256,512]{1,0:T(8,128)} custom-call(s32[2]{0:T(128)S(1)} %pad_add_fusion.refs_0_, f32[16,2,16,512]{3,2,1,0:T(8,128)S(1)} %bitcast.15, f32[16,2,16,512]{3,2,1,0:T(8,128)S(1)} %bitcast.18, f32[256,512]{1,0:T(8,128)S(1)} %copy-done.2, f32[512,512]{1,0:T(8,128)S(1)} %copy-done.1), custom_call_target="tpu_custom_call" | custom-call | flops 805306368 | bytes 4194304 | tf_op jit(solution)/shard_map/last/pallas_call | solution.py:79
  (4 shorter events, 0.1 us)
Async XLA Ops:
  0.0 1.0 copy-start
  28.2 19.2 %collective-permute-start.1 = (f32[16,512]{1,0:T(8,128)S(1)}, f32[16,512]{1,0:T(8,128)S(1)}, u32[]{:S(2)}, u32[]{:S(2)}) collective-permute-start(f32[16,512]{1,0:T(8,128)S(1)} %reduce_sum.18), channel_id=1, source_target_pairs={{16,272},{48,273},{80,274},{112,275},{144,276},{176,277},{208,278}... | collective-permute-start | bytes 98312 | tf_op jit(solution)/shard_map/ppermute | solution.py:124
  38.9 9.3 %collective-permute-start = (f32[16,512]{1,0:T(8,128)S(1)}, f32[16,512]{1,0:T(8,128)S(1)}, u32[]{:S(2)}, u32[]{:S(2)}) collective-permute-start(f32[16,512]{1,0:T(8,128)S(1)} %reduce_sum.18), channel_id=1, source_target_pairs={{0,272},{32,273},{64,274},{96,275},{128,276},{160,277},{192,278},{... | collective-permute-start | bytes 98312 | tf_op jit(solution)/shard_map/ppermute | solution.py:124
  48.3 27.7 %copy-start.1 = (f32[512,512]{1,0:T(8,128)S(1)}, f32[512,512]{1,0:T(8,128)}, u32[]{:S(2)}) copy-start(f32[512,512]{1,0:T(8,128)} %refs_4_.3) | copy-start | bytes 3145732
  48.3 27.7 %copy-start.2 = (f32[256,512]{1,0:T(8,128)S(1)}, f32[256,512]{1,0:T(8,128)}, u32[]{:S(2)}) copy-start(f32[256,512]{1,0:T(8,128)} %refs_3_.3) | copy-start | bytes 1572868
  71.3 4.7 %collective-permute-start.2 = (f32[512,512]{1,0:T(8,128)S(1)}, f32[512,512]{1,0:T(8,128)S(1)}, u32[]{:S(2)}, u32[]{:S(2)}) collective-permute-start(f32[512,512]{1,0:T(8,128)S(1)} %bitcast.12), channel_id=1, source_target_pairs={{0,16},{16,0},{32,48},{48,32},{64,80},{80,64},{96,112},{112,96},{1... | collective-permute-start | bytes 3145736 | tf_op jit(solution)/shard_map/ppermute | solution.py:128
  98.3 14.0 %collective-permute-start.4 = (f32[16,512]{1,0:T(8,128)S(1)}, f32[16,512]{1,0:T(8,128)S(1)}, u32[]{:S(2)}, u32[]{:S(2)}) collective-permute-start(f32[16,512]{1,0:T(8,128)S(1)} %reduce_sum.19), channel_id=1, source_target_pairs={{16,272},{48,273},{80,274},{112,275},{144,276},{176,277},{208,278}... | collective-permute-start | bytes 98312 | tf_op jit(solution)/shard_map/ppermute | solution.py:124
  103.9 9.1 %collective-permute-start.3 = (f32[16,512]{1,0:T(8,128)S(1)}, f32[16,512]{1,0:T(8,128)S(1)}, u32[]{:S(2)}, u32[]{:S(2)}) collective-permute-start(f32[16,512]{1,0:T(8,128)S(1)} %reduce_sum.19), channel_id=1, source_target_pairs={{0,272},{32,273},{64,274},{96,275},{128,276},{160,277},{192,278},{... | collective-permute-start | bytes 98312 | tf_op jit(solution)/shard_map/ppermute | solution.py:124
  135.8 4.5 %collective-permute-start.5 = (f32[512,512]{1,0:T(8,128)S(1)}, f32[512,512]{1,0:T(8,128)S(1)}, u32[]{:S(2)}, u32[]{:S(2)}) collective-permute-start(f32[512,512]{1,0:T(8,128)S(1)} %bitcast.14), channel_id=1, source_target_pairs={{0,16},{16,0},{32,48},{48,32},{64,80},{80,64},{96,112},{112,96},{1... | collective-permute-start | bytes 3145736 | tf_op jit(solution)/shard_map/ppermute | solution.py:128
where the time goes:
time: 143 us
  blocking collectives  105 us (73%)
  starting transfers between devices  23.2 us (16%)
  waiting for transfers between devices  6.34 us (4%)
  Pallas kernels  4.02 us (3%)
  matrix products  1.98 us (1%)
    all_to_all x4, blocking collectives, spread(): lax.all_to_all(block, axis, split_axis=0, concat_axis=0, axis_index_group...  91.1 us
    ppermute x4, starting transfers between devices, local(): turned.append(lax.ppermute(piece, ('row', 'col'), turn[e]))  18.9 us
    all_gather x2, blocking collectives, local(): lax.all_gather(piece, 'row', axis=0, axis_index_groups=team, tiled=True)  14.3 us
    ppermute x2, waiting for transfers between devices, local(): other = lax.ppermute(got, 'row', partner)  4.81 us
    ppermute x2, starting transfers between devices, local(): other = lax.ppermute(got, 'row', partner)  4.3 us
    pallas_call x2, Pallas kernels, middle_part(): pl.pallas_call(lambda *refs: middle_kernel(scale, last, *refs), out_shape...  4.02 us
  transfers between devices with their start and end apart: 6, of which 4 were waited for; matrix products, arithmetic and copies ran while one was open for 0% of the time, Pallas kernels for 0%

commit v1 on v0

--- a/solution.py
+++ b/solution.py
@@ -31,7 +31,7 @@
     return dot(left[0], right[0]) + (dot(left[0], right[1]) + dot(left[1], right[0]))
 
 
-def middle_kernel(scale, last, info, got, other, den, factor, out, rh, rl, ch, cl, ah, al):
+def middle_kernel(scale, last, info, got, other, den, factor, out, rh, rl, ch, cl, *more):
     rows, thin = out.shape[0], got.shape[2]
 
     def sort(cols, mine, e):
@@ -50,14 +50,24 @@
     def _():
         sort(got, other, 1)
 
-    left = rh[...], rl[...]
-    for at in range(0, ch.shape[0], WIDE):
-        cols = slice(at, at + WIDE)
-        amp = product(left, (ch[cols, :], cl[cols, :]), True) / den[:, cols]
-        if last:
-            out[:, cols] = amp
-        else:
-            ah[:, cols], al[:, cols] = halves(amp)
+    if last:
+        held, sems = more
+        half = rows // 2
+        right = ch[...], cl[...]
+        stores = []
+        for n in range(2):
+            here = slice(n * half, (n + 1) * half)
+            held[here, :] = product((rh[here, :], rl[here, :]), right, True) / den[here, :]
+            stores.append(pltpu.make_async_copy(held.at[here, :], out.at[here, :], sems.at[n]))
+            stores[n].start()
+        for store in stores:
+            store.wait()
+    else:
+        ah, al = more
+        left = rh[...], rl[...]
+        for at in range(0, ch.shape[0], WIDE):
+            cols = slice(at, at + WIDE)
+            ah[:, cols], al[:, cols] = halves(product(left, (ch[cols, :], cl[cols, :]), True) / den[:, cols])
     if not last:
         left = ah[...], al[...]
         for at in range(0, out.shape[1], WIDE):
@@ -76,12 +86,13 @@
     short = pltpu.VMEM((rows, depth), jnp.bfloat16)
     tall = pltpu.VMEM((cols, depth), jnp.bfloat16)
     wide = pltpu.VMEM((rows, cols), jnp.bfloat16)
+    more = [pltpu.VMEM((rows, cols), jnp.float32), pltpu.SemaphoreType.DMA((2,))] if last else [wide, wide]
     return pl.pallas_call(
         lambda *refs: middle_kernel(scale, last, *refs),
         out_shape=jax.ShapeDtypeStruct((rows, cols if last else depth), jnp.float32),
         in_specs=[pl.BlockSpec(memory_space=pltpu.SMEM), vmem, vmem, vmem, vmem],
-        out_specs=vmem,
-        scratch_shapes=[short, short, tall, tall, wide, wide],
+        out_specs=pl.BlockSpec(memory_space=pl.ANY) if last else vmem,
+        scratch_shapes=[short, short, tall, tall, *more],
         compiler_params=pltpu.CompilerParams(vmem_limit_bytes=20 << 20),
         cost_estimate=pl.CostEstimate(flops=12 * rows * depth * cols, bytes_accessed=4 << 20, transcendentals=0),
         name="last" if last else "middle",
@@ -101,11 +112,7 @@
     info = jnp.stack([here_row % CORES, here_row // CORES == here_col]).astype(jnp.int32)
     team = [[k * CORES + e for e in range(CORES)] for k in range(ncol)]
     partner = [(r, r ^ 1) for r in range(nrow)]
-    order = []
-    for u in range(PAIR):
-        for n in range(line):
-            y = (n // 2 + (n + u) % 2 * (line // 2)) % line
-            order.append(y * PAIR + u)
+    order = [y * PAIR + u for u in range(PAIR) for y in range(line)]
     place = [(c // PAIR + line // 2) % line * PAIR + c % PAIR for c in order]
     turn = [[] for _ in range(CORES)]
     for e in range(CORES):

time: 143 us -> 142 us (level)
  blocking collectives: 105 us -> 101 us
  starting transfers between devices: 23.2 us -> 24.8 us
    all_to_all x4, blocking collectives: 91.1 us -> 88.2 us  [spread(): lax.all_to_all(block, axis, split_axis=0, concat_axis=0, axis_index_group...]
    ppermute x2, starting transfers between devices: 4.3 us -> 6.86 us  [local(): other = lax.ppermute(got, 'row', partner)]
where the time goes in v1:
time: 142 us; the launch traced here: 141 us
  blocking collectives  101 us (71%)
  starting transfers between devices  24.8 us (17%)
  waiting for transfers between devices  7.1 us (5%)
  Pallas kernels  4.47 us (3%)
  matrix products  1.98 us (1%)
    all_to_all x4, blocking collectives, spread(): lax.all_to_all(block, axis, split_axis=0, concat_axis=0, axis_index_group...  88.2 us
    ppermute x4, starting transfers between devices, local(): turned.append(lax.ppermute(piece, ('row', 'col'), turn[e]))  17.9 us
    all_gather x2, blocking collectives, local(): lax.all_gather(piece, 'row', axis=0, axis_index_groups=team, tiled=True)  13.1 us
    ppermute x2, starting transfers between devices, local(): other = lax.ppermute(got, 'row', partner)  6.86 us
    pallas_call x2, Pallas kernels, middle_part(): pl.pallas_call(lambda *refs: middle_kernel(scale, last, *refs), out_shape...  4.47 us
    ppermute x2, waiting for transfers between devices, local(): other = lax.ppermute(got, 'row', partner)  4.45 us
  transfers between devices with their start and end apart: 6, of which 4 were waited for; matrix products, arithmetic and copies ran while one was open for 0% of the time, Pallas kernels for 0%

profile of v1, /device:TPU:1, one launch (start us, length us, event | category | flops | bytes accessed | tf_op | source)
XLA Modules:
  0.0 141.2 jit_solution(9163042566321718132)
XLA Ops:
  0.0 0.0 copy-start
  0.0 1.0 copy-done
  1.0 2.0 %fusion = f32[256,512]{1,0:T(8,128)S(1)} fusion(f32[256,512]{1,0:T(8,128)S(1)} %copy-done, f32[512,512]{1,0:T(8,128)} %refs_4_.3, s32[]{:T(128)S(6)} %select_n.40, pred[]{:T(512)S(6)} %eq.14), kind=kOutput, calls=%fused_computation.1 | convolution fusion | flops 403046400 | bytes 2621445 | tf_op jit(solution)/shard_map/dot_general | solution.py:125
  3.0 25.0 %all_to_all.36 = f32[16,16,512]{2,1,0:T(8,128)S(1)} all-to-all(f32[16,16,512]{2,1,0:T(8,128)S(1)} %bitcast.19), channel_id=1, replica_groups={{0,2,4,6,8,10,12,14,1,3,5,7,9,11,13,15},{16,18,20,22,24,26,28,30,17,19,..., dimensions={0} | all-to-all | bytes 1048576 | tf_op jit(solution)/shard_map/all_to_all | solution.py:17
  28.1 10.6 %collective-permute-start.1 = (f32[16,512]{1,0:T(8,128)S(1)}, f32[16,512]{1,0:T(8,128)S(1)}, u32[]{:S(2)}, u32[]{:S(2)}) collective-permute-start(f32[16,512]{1,0:T(8,128)S(1)} %reduce_sum.18), channel_id=1, source_target_pairs={{16,272},{48,273},{80,274},{112,275},{144,276},{176,277},{208,278}... | collective-permute-start | bytes 98312 | tf_op jit(solution)/shard_map/ppermute | solution.py:131
  38.7 1.3 collective-permute-start
  40.0 6.4 %all_gather.6 = f32[32,512]{1,0:T(8,128)S(1)} all-gather(f32[16,512]{1,0:T(8,128)S(1)} %reduce_sum.18), channel_id=1, replica_groups={{0,16},{32,48},{64,80},{96,112},{128,144},{160,176},{192,208},{224,240}..., dimensions={0}, use_global_device_ids=true | all-gather | bytes 98304 | tf_op jit(solution)/shard_map/all_gather | solution.py:132
  46.4 0.0 collective-permute-done.1
  46.4 1.4 %collective-permute-done = f32[16,512]{1,0:T(8,128)S(1)} collective-permute-done((f32[16,512]{1,0:T(8,128)S(1)}, f32[16,512]{1,0:T(8,128)S(1)}, u32[]{:S(2)}, u32[]{:S(2)}) %collective-permute-start) | collective-permute-done | bytes 32800 | tf_op jit(solution)/shard_map/ppermute | solution.py:131
  47.9 0.1 tile.4
  48.0 0.0 copy-start.1
  48.0 0.0 copy-start.2
  48.0 22.3 %all_to_all.37 = f32[16,32,512]{2,1,0:T(8,128)S(1)} all-to-all(f32[16,32,512]{2,1,0:T(8,128)S(1)} %tile.4), channel_id=1, replica_groups={{0,2,4,6,8,10,12,14,1,3,5,7,9,11,13,15},{32,34,36,38,40,42,44,46,33,35,..., dimensions={0} | all-to-all | bytes 2097152 | tf_op jit(solution)/shard_map/all_to_all | solution.py:17
  70.3 3.4 %collective-permute-start.2 = (f32[512,512]{1,0:T(8,128)S(1)}, f32[512,512]{1,0:T(8,128)S(1)}, u32[]{:S(2)}, u32[]{:S(2)}) collective-permute-start(f32[512,512]{1,0:T(8,128)S(1)} %bitcast.12), channel_id=1, source_target_pairs={{0,16},{16,0},{32,48},{48,32},{64,80},{80,64},{96,112},{112,96},{1... | collective-permute-start | bytes 3145736 | tf_op jit(solution)/shard_map/ppermute | solution.py:135
  73.7 0.1 pad_add_fusion.refs_0_
  73.8 2.2 %collective-permute-done.2 = f32[512,512]{1,0:T(8,128)S(1)} collective-permute-done((f32[512,512]{1,0:T(8,128)S(1)}, f32[512,512]{1,0:T(8,128)S(1)}, u32[]{:S(2)}, u32[]{:S(2)}) %collective-permute-start.2) | collective-permute-done | bytes 1048608 | tf_op jit(solution)/shard_map/ppermute | solution.py:135
  76.0 0.0 copy-done.1
  76.0 0.0 copy-done.2
  76.0 1.9 %middle.1 = f32[256,512]{1,0:T(8,128)S(1)} custom-call(s32[2]{0:T(128)S(1)} %pad_add_fusion.refs_0_, f32[16,2,16,512]{3,2,1,0:T(8,128)S(1)} %bitcast.13, f32[16,2,16,512]{3,2,1,0:T(8,128)S(1)} %bitcast.17, f32[256,512]{1,0:T(8,128)S(1)} %copy-done.2, f32[512,512]{1,0:T(8,128)S(1)} %copy-done.1), custom_call_target="tpu_custom_call" | custom-call | flops 805306368 | bytes 4194304 | tf_op jit(solution)/shard_map/middle/pallas_call | solution.py:90
  77.9 19.3 %all_to_all.38 = f32[16,16,512]{2,1,0:T(8,128)S(1)} all-to-all(f32[16,16,512]{2,1,0:T(8,128)S(1)} %bitcast.16), channel_id=1, replica_groups={{0,2,4,6,8,10,12,14,1,3,5,7,9,11,13,15},{16,18,20,22,24,26,28,30,17,19,..., dimensions={0} | all-to-all | bytes 1048576 | tf_op jit(solution)/shard_map/all_to_all | solution.py:17
  97.2 4.7 %collective-permute-start.4 = (f32[16,512]{1,0:T(8,128)S(1)}, f32[16,512]{1,0:T(8,128)S(1)}, u32[]{:S(2)}, u32[]{:S(2)}) collective-permute-start(f32[16,512]{1,0:T(8,128)S(1)} %reduce_sum.19), channel_id=1, source_target_pairs={{16,272},{48,273},{80,274},{112,275},{144,276},{176,277},{208,278}... | collective-permute-start | bytes 98312 | tf_op jit(solution)/shard_map/ppermute | solution.py:131
  101.9 1.3 collective-permute-start.3
  103.2 6.7 %all_gather.7 = f32[32,512]{1,0:T(8,128)S(1)} all-gather(f32[16,512]{1,0:T(8,128)S(1)} %reduce_sum.19), channel_id=1, replica_groups={{0,16},{32,48},{64,80},{96,112},{128,144},{160,176},{192,208},{224,240}..., dimensions={0}, use_global_device_ids=true | all-gather | bytes 98304 | tf_op jit(solution)/shard_map/all_gather | solution.py:132
  109.9 0.0 collective-permute-done.4
  109.9 1.2 collective-permute-done.3
  111.1 0.1 tile.5
  111.2 21.6 %all_to_all.39 = f32[16,32,512]{2,1,0:T(8,128)S(1)} all-to-all(f32[16,32,512]{2,1,0:T(8,128)S(1)} %tile.5), channel_id=1, replica_groups={{0,2,4,6,8,10,12,14,1,3,5,7,9,11,13,15},{32,34,36,38,40,42,44,46,33,35,..., dimensions={0} | all-to-all | bytes 2097152 | tf_op jit(solution)/shard_map/all_to_all | solution.py:17
  132.9 3.4 %collective-permute-start.5 = (f32[512,512]{1,0:T(8,128)S(1)}, f32[512,512]{1,0:T(8,128)S(1)}, u32[]{:S(2)}, u32[]{:S(2)}) collective-permute-start(f32[512,512]{1,0:T(8,128)S(1)} %bitcast.14), channel_id=1, source_target_pairs={{0,16},{16,0},{32,48},{48,32},{64,80},{80,64},{96,112},{112,96},{1... | collective-permute-start | bytes 3145736 | tf_op jit(solution)/shard_map/ppermute | solution.py:135
  136.3 2.3 %collective-permute-done.5 = f32[512,512]{1,0:T(8,128)S(1)} collective-permute-done((f32[512,512]{1,0:T(8,128)S(1)}, f32[512,512]{1,0:T(8,128)S(1)}, u32[]{:S(2)}, u32[]{:S(2)}) %collective-permute-start.5) | collective-permute-done | bytes 1048608 | tf_op jit(solution)/shard_map/ppermute | solution.py:135
  138.6 2.6 %last.1 = f32[256,512]{1,0:T(8,128)} custom-call(s32[2]{0:T(128)S(1)} %pad_add_fusion.refs_0_, f32[16,2,16,512]{3,2,1,0:T(8,128)S(1)} %bitcast.15, f32[16,2,16,512]{3,2,1,0:T(8,128)S(1)} %bitcast.18, f32[256,512]{1,0:T(8,128)S(1)} %copy-done.2, f32[512,512]{1,0:T(8,128)S(1)} %copy-done.1), custom_call_target="tpu_custom_call" | custom-call | flops 805306368 | bytes 4194304 | tf_op jit(solution)/shard_map/last/pallas_call | solution.py:90
  (4 shorter events, 0.1 us)
Async XLA Ops:
  0.0 1.0 copy-start
  28.1 18.3 %collective-permute-start.1 = (f32[16,512]{1,0:T(8,128)S(1)}, f32[16,512]{1,0:T(8,128)S(1)}, u32[]{:S(2)}, u32[]{:S(2)}) collective-permute-start(f32[16,512]{1,0:T(8,128)S(1)} %reduce_sum.18), channel_id=1, source_target_pairs={{16,272},{48,273},{80,274},{112,275},{144,276},{176,277},{208,278}... | collective-permute-start | bytes 98312 | tf_op jit(solution)/shard_map/ppermute | solution.py:131
  38.7 9.1 %collective-permute-start = (f32[16,512]{1,0:T(8,128)S(1)}, f32[16,512]{1,0:T(8,128)S(1)}, u32[]{:S(2)}, u32[]{:S(2)}) collective-permute-start(f32[16,512]{1,0:T(8,128)S(1)} %reduce_sum.18), channel_id=1, source_target_pairs={{0,272},{32,273},{64,274},{96,275},{128,276},{160,277},{192,278},{... | collective-permute-start | bytes 98312 | tf_op jit(solution)/shard_map/ppermute | solution.py:131
  48.0 28.0 %copy-start.1 = (f32[512,512]{1,0:T(8,128)S(1)}, f32[512,512]{1,0:T(8,128)}, u32[]{:S(2)}) copy-start(f32[512,512]{1,0:T(8,128)} %refs_4_.3) | copy-start | bytes 3145732
  48.0 28.0 %copy-start.2 = (f32[256,512]{1,0:T(8,128)S(1)}, f32[256,512]{1,0:T(8,128)}, u32[]{:S(2)}) copy-start(f32[256,512]{1,0:T(8,128)} %refs_3_.3) | copy-start | bytes 1572868
  70.3 5.7 %collective-permute-start.2 = (f32[512,512]{1,0:T(8,128)S(1)}, f32[512,512]{1,0:T(8,128)S(1)}, u32[]{:S(2)}, u32[]{:S(2)}) collective-permute-start(f32[512,512]{1,0:T(8,128)S(1)} %bitcast.12), channel_id=1, source_target_pairs={{0,16},{16,0},{32,48},{48,32},{64,80},{80,64},{96,112},{112,96},{1... | collective-permute-start | bytes 3145736 | tf_op jit(solution)/shard_map/ppermute | solution.py:135
  97.2 12.7 %collective-permute-start.4 = (f32[16,512]{1,0:T(8,128)S(1)}, f32[16,512]{1,0:T(8,128)S(1)}, u32[]{:S(2)}, u32[]{:S(2)}) collective-permute-start(f32[16,512]{1,0:T(8,128)S(1)} %reduce_sum.19), channel_id=1, source_target_pairs={{16,272},{48,273},{80,274},{112,275},{144,276},{176,277},{208,278}... | collective-permute-start | bytes 98312 | tf_op jit(solution)/shard_map/ppermute | solution.py:131
  101.9 9.2 %collective-permute-start.3 = (f32[16,512]{1,0:T(8,128)S(1)}, f32[16,512]{1,0:T(8,128)S(1)}, u32[]{:S(2)}, u32[]{:S(2)}) collective-permute-start(f32[16,512]{1,0:T(8,128)S(1)} %reduce_sum.19), channel_id=1, source_target_pairs={{0,272},{32,273},{64,274},{96,275},{128,276},{160,277},{192,278},{... | collective-permute-start | bytes 98312 | tf_op jit(solution)/shard_map/ppermute | solution.py:131
  132.9 5.7 %collective-permute-start.5 = (f32[512,512]{1,0:T(8,128)S(1)}, f32[512,512]{1,0:T(8,128)S(1)}, u32[]{:S(2)}, u32[]{:S(2)}) collective-permute-start(f32[512,512]{1,0:T(8,128)S(1)} %bitcast.14), channel_id=1, source_target_pairs={{0,16},{16,0},{32,48},{48,32},{64,80},{80,64},{96,112},{112,96},{1... | collective-permute-start | bytes 3145736 | tf_op jit(solution)/shard_map/ppermute | solution.py:135

commit v2 on v0

--- a/solution.py
+++ b/solution.py
@@ -8,7 +8,7 @@
 from jax.sharding import PartitionSpec as P
 
 ITERS = 2
-WIDE = 256
+WIDE = 512
 PAIR = 2
 CORES = 2
 
@@ -101,11 +101,7 @@
     info = jnp.stack([here_row % CORES, here_row // CORES == here_col]).astype(jnp.int32)
     team = [[k * CORES + e for e in range(CORES)] for k in range(ncol)]
     partner = [(r, r ^ 1) for r in range(nrow)]
-    order = []
-    for u in range(PAIR):
-        for n in range(line):
-            y = (n // 2 + (n + u) % 2 * (line // 2)) % line
-            order.append(y * PAIR + u)
+    order = [y * PAIR + u for u in range(PAIR) for y in range(line)]
     place = [(c // PAIR + line // 2) % line * PAIR + c % PAIR for c in order]
     turn = [[] for _ in range(CORES)]
     for e in range(CORES):

time: 143 us -> 141 us (0.986)
  blocking collectives: 105 us -> 101 us
  starting transfers between devices: 23.2 us -> 24.8 us
    all_to_all x4, blocking collectives: 91.1 us -> 88.2 us  [spread(): lax.all_to_all(block, axis, split_axis=0, concat_axis=0, axis_index_group...]
    ppermute x2, starting transfers between devices: 4.3 us -> 6.86 us  [local(): other = lax.ppermute(got, 'row', partner)]
where the time goes in v2:
time: 141 us
  blocking collectives  101 us (72%)
  starting transfers between devices  24.8 us (18%)
  waiting for transfers between devices  7.1 us (5%)
  Pallas kernels  4.01 us (3%)
  matrix products  1.98 us (1%)
    all_to_all x4, blocking collectives, spread(): lax.all_to_all(block, axis, split_axis=0, concat_axis=0, axis_index_group...  88.2 us
    ppermute x4, starting transfers between devices, local(): turned.append(lax.ppermute(piece, ('row', 'col'), turn[e]))  17.9 us
    all_gather x2, blocking collectives, local(): lax.all_gather(piece, 'row', axis=0, axis_index_groups=team, tiled=True)  13.1 us
    ppermute x2, starting transfers between devices, local(): other = lax.ppermute(got, 'row', partner)  6.86 us
    ppermute x2, waiting for transfers between devices, local(): other = lax.ppermute(got, 'row', partner)  4.45 us
    pallas_call x2, Pallas kernels, middle_part(): pl.pallas_call(lambda *refs: middle_kernel(scale, last, *refs), out_shape...  4.01 us
  transfers between devices with their start and end apart: 6, of which 4 were waited for; matrix products, arithmetic and copies ran while one was open for 0% of the time, Pallas kernels for 0%

profile of v2, /device:TPU:1, one launch (start us, length us, event | category | flops | bytes accessed | tf_op | source)
XLA Modules:
  0.0 140.7 jit_solution(14088259411644874507)
XLA Ops:
  0.0 0.0 copy-start
  0.0 1.0 copy-done
  1.0 2.0 %fusion = f32[256,512]{1,0:T(8,128)S(1)} fusion(f32[256,512]{1,0:T(8,128)S(1)} %copy-done, f32[512,512]{1,0:T(8,128)} %refs_4_.3, s32[]{:T(128)S(6)} %select_n.40, pred[]{:T(512)S(6)} %eq.14), kind=kOutput, calls=%fused_computation.1 | convolution fusion | flops 403046400 | bytes 2621445 | tf_op jit(solution)/shard_map/dot_general | solution.py:114
  3.0 25.0 %all_to_all.36 = f32[16,16,512]{2,1,0:T(8,128)S(1)} all-to-all(f32[16,16,512]{2,1,0:T(8,128)S(1)} %bitcast.19), channel_id=1, replica_groups={{0,2,4,6,8,10,12,14,1,3,5,7,9,11,13,15},{16,18,20,22,24,26,28,30,17,19,..., dimensions={0} | all-to-all | bytes 1048576 | tf_op jit(solution)/shard_map/all_to_all | solution.py:17
  28.1 10.6 %collective-permute-start.1 = (f32[16,512]{1,0:T(8,128)S(1)}, f32[16,512]{1,0:T(8,128)S(1)}, u32[]{:S(2)}, u32[]{:S(2)}) collective-permute-start(f32[16,512]{1,0:T(8,128)S(1)} %reduce_sum.18), channel_id=1, source_target_pairs={{16,272},{48,273},{80,274},{112,275},{144,276},{176,277},{208,278}... | collective-permute-start | bytes 98312 | tf_op jit(solution)/shard_map/ppermute | solution.py:120
  38.7 1.3 collective-permute-start
  40.0 6.4 %all_gather.6 = f32[32,512]{1,0:T(8,128)S(1)} all-gather(f32[16,512]{1,0:T(8,128)S(1)} %reduce_sum.18), channel_id=1, replica_groups={{0,16},{32,48},{64,80},{96,112},{128,144},{160,176},{192,208},{224,240}..., dimensions={0}, use_global_device_ids=true | all-gather | bytes 98304 | tf_op jit(solution)/shard_map/all_gather | solution.py:121
  46.4 0.0 collective-permute-done.1
  46.4 1.4 %collective-permute-done = f32[16,512]{1,0:T(8,128)S(1)} collective-permute-done((f32[16,512]{1,0:T(8,128)S(1)}, f32[16,512]{1,0:T(8,128)S(1)}, u32[]{:S(2)}, u32[]{:S(2)}) %collective-permute-start) | collective-permute-done | bytes 32800 | tf_op jit(solution)/shard_map/ppermute | solution.py:120
  47.9 0.1 tile.4
  48.0 0.0 copy-start.1
  48.0 0.0 copy-start.2
  48.0 22.3 %all_to_all.37 = f32[16,32,512]{2,1,0:T(8,128)S(1)} all-to-all(f32[16,32,512]{2,1,0:T(8,128)S(1)} %tile.4), channel_id=1, replica_groups={{0,2,4,6,8,10,12,14,1,3,5,7,9,11,13,15},{32,34,36,38,40,42,44,46,33,35,..., dimensions={0} | all-to-all | bytes 2097152 | tf_op jit(solution)/shard_map/all_to_all | solution.py:17
  70.3 3.4 %collective-permute-start.2 = (f32[512,512]{1,0:T(8,128)S(1)}, f32[512,512]{1,0:T(8,128)S(1)}, u32[]{:S(2)}, u32[]{:S(2)}) collective-permute-start(f32[512,512]{1,0:T(8,128)S(1)} %bitcast.12), channel_id=1, source_target_pairs={{0,16},{16,0},{32,48},{48,32},{64,80},{80,64},{96,112},{112,96},{1... | collective-permute-start | bytes 3145736 | tf_op jit(solution)/shard_map/ppermute | solution.py:124
  73.7 0.1 pad_add_fusion.refs_0_
  73.8 2.2 %collective-permute-done.2 = f32[512,512]{1,0:T(8,128)S(1)} collective-permute-done((f32[512,512]{1,0:T(8,128)S(1)}, f32[512,512]{1,0:T(8,128)S(1)}, u32[]{:S(2)}, u32[]{:S(2)}) %collective-permute-start.2) | collective-permute-done | bytes 1048608 | tf_op jit(solution)/shard_map/ppermute | solution.py:124
  76.0 0.0 copy-done.1
  76.0 0.0 copy-done.2
  76.0 1.9 %middle.1 = f32[256,512]{1,0:T(8,128)S(1)} custom-call(s32[2]{0:T(128)S(1)} %pad_add_fusion.refs_0_, f32[16,2,16,512]{3,2,1,0:T(8,128)S(1)} %bitcast.13, f32[16,2,16,512]{3,2,1,0:T(8,128)S(1)} %bitcast.17, f32[256,512]{1,0:T(8,128)S(1)} %copy-done.2, f32[512,512]{1,0:T(8,128)S(1)} %copy-done.1), custom_call_target="tpu_custom_call" | custom-call | flops 805306368 | bytes 4194304 | tf_op jit(solution)/shard_map/middle/pallas_call | solution.py:79
  77.9 19.3 %all_to_all.38 = f32[16,16,512]{2,1,0:T(8,128)S(1)} all-to-all(f32[16,16,512]{2,1,0:T(8,128)S(1)} %bitcast.16), channel_id=1, replica_groups={{0,2,4,6,8,10,12,14,1,3,5,7,9,11,13,15},{16,18,20,22,24,26,28,30,17,19,..., dimensions={0} | all-to-all | bytes 1048576 | tf_op jit(solution)/shard_map/all_to_all | solution.py:17
  97.2 4.7 %collective-permute-start.4 = (f32[16,512]{1,0:T(8,128)S(1)}, f32[16,512]{1,0:T(8,128)S(1)}, u32[]{:S(2)}, u32[]{:S(2)}) collective-permute-start(f32[16,512]{1,0:T(8,128)S(1)} %reduce_sum.19), channel_id=1, source_target_pairs={{16,272},{48,273},{80,274},{112,275},{144,276},{176,277},{208,278}... | collective-permute-start | bytes 98312 | tf_op jit(solution)/shard_map/ppermute | solution.py:120
  101.9 1.3 collective-permute-start.3
  103.2 6.7 %all_gather.7 = f32[32,512]{1,0:T(8,128)S(1)} all-gather(f32[16,512]{1,0:T(8,128)S(1)} %reduce_sum.19), channel_id=1, replica_groups={{0,16},{32,48},{64,80},{96,112},{128,144},{160,176},{192,208},{224,240}..., dimensions={0}, use_global_device_ids=true | all-gather | bytes 98304 | tf_op jit(solution)/shard_map/all_gather | solution.py:121
  109.9 0.0 collective-permute-done.4
  109.9 1.2 collective-permute-done.3
  111.1 0.1 tile.5
  111.2 21.6 %all_to_all.39 = f32[16,32,512]{2,1,0:T(8,128)S(1)} all-to-all(f32[16,32,512]{2,1,0:T(8,128)S(1)} %tile.5), channel_id=1, replica_groups={{0,2,4,6,8,10,12,14,1,3,5,7,9,11,13,15},{32,34,36,38,40,42,44,46,33,35,..., dimensions={0} | all-to-all | bytes 2097152 | tf_op jit(solution)/shard_map/all_to_all | solution.py:17
  132.9 3.4 %collective-permute-start.5 = (f32[512,512]{1,0:T(8,128)S(1)}, f32[512,512]{1,0:T(8,128)S(1)}, u32[]{:S(2)}, u32[]{:S(2)}) collective-permute-start(f32[512,512]{1,0:T(8,128)S(1)} %bitcast.14), channel_id=1, source_target_pairs={{0,16},{16,0},{32,48},{48,32},{64,80},{80,64},{96,112},{112,96},{1... | collective-permute-start | bytes 3145736 | tf_op jit(solution)/shard_map/ppermute | solution.py:124
  136.3 2.3 %collective-permute-done.5 = f32[512,512]{1,0:T(8,128)S(1)} collective-permute-done((f32[512,512]{1,0:T(8,128)S(1)}, f32[512,512]{1,0:T(8,128)S(1)}, u32[]{:S(2)}, u32[]{:S(2)}) %collective-permute-start.5) | collective-permute-done | bytes 1048608 | tf_op jit(solution)/shard_map/ppermute | solution.py:124
  138.6 2.1 %last.1 = f32[256,512]{1,0:T(8,128)} custom-call(s32[2]{0:T(128)S(1)} %pad_add_fusion.refs_0_, f32[16,2,16,512]{3,2,1,0:T(8,128)S(1)} %bitcast.15, f32[16,2,16,512]{3,2,1,0:T(8,128)S(1)} %bitcast.18, f32[256,512]{1,0:T(8,128)S(1)} %copy-done.2, f32[512,512]{1,0:T(8,128)S(1)} %copy-done.1), custom_call_target="tpu_custom_call" | custom-call | flops 805306368 | bytes 4194304 | tf_op jit(solution)/shard_map/last/pallas_call | solution.py:79
  (4 shorter events, 0.1 us)
Async XLA Ops:
  0.0 1.0 copy-start
  28.1 18.3 %collective-permute-start.1 = (f32[16,512]{1,0:T(8,128)S(1)}, f32[16,512]{1,0:T(8,128)S(1)}, u32[]{:S(2)}, u32[]{:S(2)}) collective-permute-start(f32[16,512]{1,0:T(8,128)S(1)} %reduce_sum.18), channel_id=1, source_target_pairs={{16,272},{48,273},{80,274},{112,275},{144,276},{176,277},{208,278}... | collective-permute-start | bytes 98312 | tf_op jit(solution)/shard_map/ppermute | solution.py:120
  38.7 9.1 %collective-permute-start = (f32[16,512]{1,0:T(8,128)S(1)}, f32[16,512]{1,0:T(8,128)S(1)}, u32[]{:S(2)}, u32[]{:S(2)}) collective-permute-start(f32[16,512]{1,0:T(8,128)S(1)} %reduce_sum.18), channel_id=1, source_target_pairs={{0,272},{32,273},{64,274},{96,275},{128,276},{160,277},{192,278},{... | collective-permute-start | bytes 98312 | tf_op jit(solution)/shard_map/ppermute | solution.py:120
  48.0 28.0 %copy-start.1 = (f32[512,512]{1,0:T(8,128)S(1)}, f32[512,512]{1,0:T(8,128)}, u32[]{:S(2)}) copy-start(f32[512,512]{1,0:T(8,128)} %refs_4_.3) | copy-start | bytes 3145732
  48.0 28.0 %copy-start.2 = (f32[256,512]{1,0:T(8,128)S(1)}, f32[256,512]{1,0:T(8,128)}, u32[]{:S(2)}) copy-start(f32[256,512]{1,0:T(8,128)} %refs_3_.3) | copy-start | bytes 1572868
  70.3 5.7 %collective-permute-start.2 = (f32[512,512]{1,0:T(8,128)S(1)}, f32[512,512]{1,0:T(8,128)S(1)}, u32[]{:S(2)}, u32[]{:S(2)}) collective-permute-start(f32[512,512]{1,0:T(8,128)S(1)} %bitcast.12), channel_id=1, source_target_pairs={{0,16},{16,0},{32,48},{48,32},{64,80},{80,64},{96,112},{112,96},{1... | collective-permute-start | bytes 3145736 | tf_op jit(solution)/shard_map/ppermute | solution.py:124
  97.2 12.7 %collective-permute-start.4 = (f32[16,512]{1,0:T(8,128)S(1)}, f32[16,512]{1,0:T(8,128)S(1)}, u32[]{:S(2)}, u32[]{:S(2)}) collective-permute-start(f32[16,512]{1,0:T(8,128)S(1)} %reduce_sum.19), channel_id=1, source_target_pairs={{16,272},{48,273},{80,274},{112,275},{144,276},{176,277},{208,278}... | collective-permute-start | bytes 98312 | tf_op jit(solution)/shard_map/ppermute | solution.py:120
  101.9 9.2 %collective-permute-start.3 = (f32[16,512]{1,0:T(8,128)S(1)}, f32[16,512]{1,0:T(8,128)S(1)}, u32[]{:S(2)}, u32[]{:S(2)}) collective-permute-start(f32[16,512]{1,0:T(8,128)S(1)} %reduce_sum.19), channel_id=1, source_target_pairs={{0,272},{32,273},{64,274},{96,275},{128,276},{160,277},{192,278},{... | collective-permute-start | bytes 98312 | tf_op jit(solution)/shard_map/ppermute | solution.py:120
  132.9 5.7 %collective-permute-start.5 = (f32[512,512]{1,0:T(8,128)S(1)}, f32[512,512]{1,0:T(8,128)S(1)}, u32[]{:S(2)}, u32[]{:S(2)}) collective-permute-start(f32[512,512]{1,0:T(8,128)S(1)} %bitcast.14), channel_id=1, source_target_pairs={{0,16},{16,0},{32,48},{48,32},{64,80},{80,64},{96,112},{112,96},{1... | collective-permute-start | bytes 3145736 | tf_op jit(solution)/shard_map/ppermute | solution.py:124
